TPU v7x, 32 devices: a whole 2x2x4 slice. The times are simulated.
32 devices in a mesh: tm: 4 (over x, core), rows: 8 (over z, y).
Axes of the slice: x: 2, y: 2, z: 4, core: 2. Of those that a mesh axis runs over, the one named last changes fastest.
Arguments:
- smoother_gains: bfloat16 [4, 1536, 1536], P('tm', 'rows'), may hold values from -1 to 1
- smoother_offsets: bfloat16 [4, 1536], P('tm', 'rows'), may hold values from -6 to 6
- smoother_covs: bfloat16 [4, 1536, 1536], P('tm', 'rows'), may hold values from -1 to 4, as said below
Outputs:
- smoothed_means: bfloat16 [4, 1536], P('tm', 'rows')
- smoothed_covs: bfloat16 [4, 1536, 1536], P('tm', 'rows')
Inputs may be any that keep to these rules, and one draw needn't show every extreme that they name: `smoother_covs`: each step's covariance matrix is symmetric.
All inputs are finite; a program needn't handle non-finite values.
Results may differ from a plain program's by a relative error of at most 0.025.
Values may be sent and summed in bfloat16 or wider, within the bound.
A program may use at most 64 MiB of HBM per device.

v0:
```python
import jax
import jax.numpy as jnp
from jax import lax
from jax.sharding import PartitionSpec as P


def from_behind(block, axis, distance):
    devices = range(lax.axis_size(axis))
    route = [(i - distance, i) for i in devices if i - distance in devices]
    return lax.ppermute(block, axis, route)


def fold_rows(left_panel, pieces):
    return tuple(
        (jnp.dot(left_panel, portion, preferred_element_type=jnp.float32) for portion in pieces)
    )


def shards(smoother_gains, smoother_offsets, smoother_covs):
    own_gain = smoother_gains[0]
    own_offset = smoother_offsets[0]
    own_cov = smoother_covs[0]
    whole_gain = lax.all_gather(own_gain, "rows", axis=0, tiled=True)
    mean_now = own_offset
    cov_now = own_cov
    for round_index in range(lax.axis_size("tm") - 1):
        mean_in, cov_in = from_behind((mean_now, cov_now), "tm", -1)
        mean_sum, left_times = fold_rows(
            own_gain,
            (
                lax.all_gather(mean_in, "rows", axis=0, tiled=True),
                lax.all_gather(cov_in, "rows", axis=0, tiled=True),
            ),
        )
        product_full = lax.dot_general(
            left_times.astype(jnp.bfloat16),
            whole_gain,
            (((1,), (1,)), ((), ())),
            preferred_element_type=jnp.float32,
        )
        mean_now = (mean_sum + own_offset.astype(jnp.float32)).astype(jnp.bfloat16)
        cov_now = (product_full + own_cov.astype(jnp.float32)).astype(jnp.bfloat16)
    return (mean_now[None], cov_now[None])


def solution(mesh):
    in_specs = (P("tm", "rows", None), P("tm", "rows"), P("tm", "rows", None))
    out_specs = (P("tm", "rows"), P("tm", "rows", None))
    return jax.shard_map(shards, mesh=mesh, in_specs=in_specs, out_specs=out_specs, check_vma=False)
```

profile of v0, /device:TPU:0, one launch (start us, length us, event | category | flops | bytes accessed | tf_op | source)
XLA Modules:
  0.0 384.1 jit_solution(2064067778634341476)
XLA Ops:
  7.2 0.0 all-gather.12.cloned.1.call-start
  7.2 0.7 all-gather.12.cloned.1.call-update
  7.9 0.0 all-gather.6.cloned.1.call-start
  7.9 1.3 collective-permute-start.3
  9.2 2.8 collective-permute-done.3
  12.1 0.8 copy-done.2
  12.9 0.0 all-gather.6.cloned.1.call-update
  12.9 0.0 copy-start
  12.9 0.0 copy-start.5
  12.9 0.0 all-gather.8.cloned.1.call-start
  13.0 79.8 %all-gather.12.cloned.1.call-done = bf16[1,1536,1536]{2,1,0:T(8,128)(2,1)} async-done(((bf16[1,192,1536]{2,1,0:T(8,128)(2,1)}), bf16[1,1536,1536]{2,1,0:T(8,128)(2,1)}) %all-gather.12.cloned.1.call-update) | async-done | bytes 4718608 | tf_op jit(solution)/shard_map/all_gather | solution.py:23
  92.8 80.8 %all-gather.6.cloned.1.call-done = bf16[1536,1536]{1,0:T(8,128)(2,1)} async-done(((bf16[192,1536]{1,0:T(8,128)(2,1)}), bf16[1536,1536]{1,0:T(8,128)(2,1)}) %all-gather.6.cloned.1.call-update) | async-done | bytes 4718608 | tf_op jit(solution)/shard_map/all_gather | solution.py:32
  173.6 6.6 %fusion.15 = bf16[192,1536]{1,0:T(8,128)(2,1)S(1)} fusion(bf16[1,1536,1536]{2,1,0:T(8,128)(2,1)} %all-gather.12.cloned.1.call-done, bf16[1536,1536]{1,0:T(8,128)(2,1)} %all-gather.6.cloned.1.call-done, bf16[1,192,1536]{2,1,0:T(8,128)(2,1)} %param.3, bf16[1,192,1536]{2,1,0:T(8,128)(2,1)} %param.5), kind=kOutput, calls=%fused_computation.12 | convolution fusion | flops 1813118976 | bytes 11206656 | tf_op jit(solution)/shard_map/dot_general | solution.py:35
  180.2 1.3 collective-permute-start.4
  181.5 2.6 collective-permute-done.4
  184.1 0.8 copy-done.3
  184.9 0.0 all-gather.8.cloned.1.call-update
  185.0 0.0 copy-start.4
  185.0 0.0 copy-start.6
  185.0 0.0 all-gather.10.cloned.1.call-start
  185.0 84.1 %all-gather.8.cloned.1.call-done = bf16[1536,1536]{1,0:T(8,128)(2,1)} async-done(((bf16[192,1536]{1,0:T(8,128)(2,1)}), bf16[1536,1536]{1,0:T(8,128)(2,1)}) %all-gather.8.cloned.1.call-update) | async-done | bytes 4718608 | tf_op jit(solution)/shard_map/all_gather | solution.py:32
  269.2 0.0 copy-done
  269.2 0.0 copy-done.5
  269.2 8.8 %fusion.21 = bf16[192,1536]{1,0:T(8,128)(2,1)S(1)} fusion(bf16[1,1536,1536]{2,1,0:T(8,128)(2,1)} %all-gather.12.cloned.1.call-done, bf16[1536,1536]{1,0:T(8,128)(2,1)} %all-gather.8.cloned.1.call-done, bf16[1,192,1536]{2,1,0:T(8,128)(2,1)S(1)} %copy-done, bf16[1,192,1536]{2,1,0:T(8,128)(2,1)S(1)} %copy-done.5), kind=kOutput, calls=%fused_computation.14 | convolution fusion | flops 1813118976 | bytes 11206656 | tf_op jit(solution)/shard_map/dot_general | solution.py:35
  278.0 1.3 collective-permute-start.5
  279.3 2.6 collective-permute-done.5
  281.9 0.8 copy-done.1
  282.7 0.0 all-gather.10.cloned.1.call-update
  282.7 0.0 copy-done.4
  282.7 1.3 collective-permute-start
  284.0 0.6 dynamic-slice
  285.3 7.1 %collective-permute-done = bf16[192]{0:T(256)(128)(2,1)S(1)} collective-permute-done((bf16[192]{0:T(256)(128)(2,1)S(1)}, bf16[192]{0:T(256)(128)(2,1)S(1)}, u32[]{:S(2)}, u32[]{:S(2)}) %collective-permute-start) | collective-permute-done | bytes 416 | tf_op jit(solution)/shard_map/ppermute | solution.py:10
  292.4 0.2 dynamic-update-slice
  292.6 19.1 %all-reduce = bf16[1536]{0:T(1024)(128)(2,1)S(1)} all-reduce(bf16[1536]{0:T(1024)(128)(2,1)S(1)} %dynamic-update-slice), channel_id=1, replica_groups=mesh['tm'=4,'rows'=8] {'rows'}, use_global_device_ids=true, to_apply=%add | all-reduce | flops 1536 | bytes 6144
  311.7 0.2 fusion.37
  312.0 1.3 collective-permute-start.1
  313.3 1.7 collective-permute-done.1
  315.0 0.2 dynamic-update-slice.1
  315.2 17.7 %all-reduce.1 = bf16[1536]{0:T(1024)(128)(2,1)S(1)} all-reduce(bf16[1536]{0:T(1024)(128)(2,1)S(1)} %dynamic-update-slice.1), channel_id=1, replica_groups=mesh['tm'=4,'rows'=8] {'rows'}, use_global_device_ids=true, to_apply=%add.1 | all-reduce | flops 1536 | bytes 6144
  332.9 0.2 fusion.35
  333.1 1.3 collective-permute-start.2
  334.5 1.7 collective-permute-done.2
  336.2 0.2 dynamic-update-slice.2
  336.4 19.7 %all-reduce.2 = bf16[1536]{0:T(1024)(128)(2,1)S(1)} all-reduce(bf16[1536]{0:T(1024)(128)(2,1)S(1)} %dynamic-update-slice.2), channel_id=1, replica_groups=mesh['tm'=4,'rows'=8] {'rows'}, use_global_device_ids=true, to_apply=%add.2 | all-reduce | flops 1536 | bytes 6144
  356.1 0.2 fusion.33
  356.4 0.6 broadcast_in_dim.6
  357.0 11.0 %all-gather.10.cloned.1.call-done = bf16[1536,1536]{1,0:T(8,128)(2,1)} async-done(((bf16[192,1536]{1,0:T(8,128)(2,1)}), bf16[1536,1536]{1,0:T(8,128)(2,1)}) %all-gather.10.cloned.1.call-update) | async-done | bytes 4718608 | tf_op jit(solution)/shard_map/all_gather | solution.py:32
  368.0 9.6 %fusion.24 = bf16[1,192,1536]{2,1,0:T(8,128)(2,1)} fusion(bf16[1,1536,1536]{2,1,0:T(8,128)(2,1)} %all-gather.12.cloned.1.call-done, bf16[1536,1536]{1,0:T(8,128)(2,1)} %all-gather.10.cloned.1.call-done, bf16[1,192,1536]{2,1,0:T(8,128)(2,1)S(1)} %copy-done, bf16[1,192,1536]{2,1,0:T(8,128)(2,1)S(1)} %copy-done.5), kind=kOutput, calls=%fused_computation.15 | convolution fusion | flops 1813118976 | bytes 11206656 | tf_op jit(solution)/shard_map/dot_general | solution.py:35
  (14 shorter events, 0.1 us)
Async XLA Ops:
  7.2 85.6 %all-gather.12.cloned.1.call-start = ((), (), s32[]{:S(2)}) async-start(), calls=%async_computation.3 | async-start | bytes 5308416 | tf_op jit(solution)/shard_map/all_gather | solution.py:23
  7.9 165.7 %all-gather.6.cloned.1.call-start = ((), (), s32[]{:S(2)}) async-start(), calls=%async_computation | async-start | bytes 5308416 | tf_op jit(solution)/shard_map/all_gather | solution.py:32
  7.9 4.1 %collective-permute-start.3 = (bf16[192,1536]{1,0:T(8,128)(2,1)}, bf16[192,1536]{1,0:T(8,128)(2,1)S(1)}, u32[]{:S(2)}, u32[]{:S(2)}) collective-permute-start(bf16[192,1536]{1,0:T(8,128)(2,1)} %bitcast.56), channel_id=1, source_target_pairs={{8,0},{16,8},{24,16},{9,1},{17,9},{25,17},{10,2},{18,10},{26,18},{... | collective-permute-start | bytes 1769480 | tf_op jit(solution)/shard_map/ppermute | solution.py:10
  12.1 0.8 copy-start.2
  12.9 256.3 %copy-start = (bf16[1,192,1536]{2,1,0:T(8,128)(2,1)S(1)}, bf16[1,192,1536]{2,1,0:T(8,128)(2,1)}, u32[]{:S(2)}) copy-start(bf16[1,192,1536]{2,1,0:T(8,128)(2,1)} %param.3) | copy-start | bytes 1769476
  12.9 256.3 %copy-start.5 = (bf16[1,192,1536]{2,1,0:T(8,128)(2,1)S(1)}, bf16[1,192,1536]{2,1,0:T(8,128)(2,1)}, u32[]{:S(2)}) copy-start(bf16[1,192,1536]{2,1,0:T(8,128)(2,1)} %param.5) | copy-start | bytes 1769476
  12.9 256.3 %all-gather.8.cloned.1.call-start = ((), (), s32[]{:S(2)}) async-start(), calls=%async_computation.1 | async-start | bytes 5308416 | tf_op jit(solution)/shard_map/all_gather | solution.py:32
  180.2 3.9 %collective-permute-start.4 = (bf16[192,1536]{1,0:T(8,128)(2,1)S(1)}, bf16[192,1536]{1,0:T(8,128)(2,1)S(1)}, u32[]{:S(2)}, u32[]{:S(2)}) collective-permute-start(bf16[192,1536]{1,0:T(8,128)(2,1)S(1)} %fusion.15), channel_id=1, source_target_pairs={{8,0},{16,8},{24,16},{9,1},{17,9},{25,17},{10,2},{18,10},{26,18},{... | collective-permute-start | bytes 1769480 | tf_op jit(solution)/shard_map/ppermute | solution.py:10
  184.1 0.8 copy-start.3
  185.0 97.7 %copy-start.4 = (bf16[1,192]{1,0:T(2,128)(2,1)S(1)}, bf16[1,192]{1,0:T(2,128)(2,1)}, u32[]{:S(2)}) copy-start(bf16[1,192]{1,0:T(2,128)(2,1)} %param.4) | copy-start | bytes 1156
  185.0 99.1 %copy-start.6 = (u32[32]{0:T(128)S(1)}, u32[32]{0:T(128)}, u32[]{:S(2)}) copy-start(u32[32]{0:T(128)} %constant.5) | copy-start | bytes 388
  185.0 183.0 %all-gather.10.cloned.1.call-start = ((), (), s32[]{:S(2)}) async-start(), calls=%async_computation.2 | async-start | bytes 5308416 | tf_op jit(solution)/shard_map/all_gather | solution.py:32
  278.0 3.9 %collective-permute-start.5 = (bf16[192,1536]{1,0:T(8,128)(2,1)S(1)}, bf16[192,1536]{1,0:T(8,128)(2,1)S(1)}, u32[]{:S(2)}, u32[]{:S(2)}) collective-permute-start(bf16[192,1536]{1,0:T(8,128)(2,1)S(1)} %fusion.21), channel_id=1, source_target_pairs={{8,0},{16,8},{24,16},{9,1},{17,9},{25,17},{10,2},{18,10},{26,18},{... | collective-permute-start | bytes 1769480 | tf_op jit(solution)/shard_map/ppermute | solution.py:10
  281.9 0.8 copy-start.1
  282.7 9.7 %collective-permute-start = (bf16[192]{0:T(256)(128)(2,1)S(1)}, bf16[192]{0:T(256)(128)(2,1)S(1)}, u32[]{:S(2)}, u32[]{:S(2)}) collective-permute-start(bf16[192]{0:T(256)(128)(2,1)S(1)} %reduce), channel_id=1, source_target_pairs={{8,0},{16,8},{24,16},{9,1},{17,9},{25,17},{10,2},{18,10},{26,18},{... | collective-permute-start | bytes 1160 | tf_op jit(solution)/shard_map/ppermute | solution.py:10
  312.0 3.0 collective-permute-start.1
  333.1 3.0 collective-permute-start.2
Sparse Core Ops, SparseCore 0:
  10.2 82.5 all-gather.11
  95.6 78.0 all-gather.5
  185.1 84.0 all-gather.7
  282.8 85.1 all-gather.9
where the time goes:
time: 384 us
  waiting for transfers between devices  275 us (72%)
  blocking collectives  56.6 us (15%)
  matrix products  25.7 us (7%)
  between operations  14.5 us (4%)
  starting transfers between devices  7.96 us (2%)
  local copies, waits for them, and re-layouts  4.25 us (1%)
    all_gather x3, waiting for transfers between devices, shards(): lax.all_gather(cov_in, 'rows', axis=0, tiled=True)  176 us
    all_gather x1, waiting for transfers between devices, shards(): whole_gain = lax.all_gather(own_gain, 'rows', axis=0, tiled=True)  79.8 us
    unnamed x3, blocking collectives  56.6 us
    dot_general x3, matrix products, shards(): lax.dot_general(left_times.astype(jnp.bfloat16), whole_gain, (((1,), (1,)...  25 us
    ppermute x6, waiting for transfers between devices, from_behind(): return lax.ppermute(block, axis, route)  18.6 us
    ppermute x6, starting transfers between devices, from_behind(): return lax.ppermute(block, axis, route)  7.8 us
  transfers between devices with their start and end apart: 10, of which 10 were waited for; matrix products, arithmetic and copies ran while one was open for 1% of the time, Pallas kernels for 0%

commit v1 on v0

v1 whole, which is shorter than its diff:
```python
import functools

import jax
import jax.numpy as jnp
from jax import lax
from jax.experimental import pallas as pl
from jax.experimental.pallas import tpu as pltpu
from jax.sharding import PartitionSpec as P

MESH = pl.DeviceIdType.MESH
CHUNKS = 3
GROUPS = 4
PAD = 16
CONTRACT_LAST = (((1,), (1,)), ((), ()))


def ring_row(place, n):
    side = place // (n // 2)
    return (1 - side) * 2 * place + side * (2 * (n - 1 - place) + 1)


def ring_place(row, n):
    odd = row % 2
    return (1 - odd) * (row // 2) + odd * (n - 1 - row // 2)


def kernel(
    steps, n, gain_in, offset_in, cov_in, mean_out, cov_out,
    gain, cov_next, left_out, left_in, left, offsets, mean_next, mean_send,
    gain_sem, ring_send, ring_recv, left_send, left_recv,
    offset_send, offset_recv, cov_send, cov_recv, mean_sems, gate,
):
    t = lax.axis_index("tm")
    r = lax.axis_index("rows")
    place = ring_place(r, n)
    rows, size = cov_in.shape
    half = rows // 2
    piece = half // CHUNKS
    part = size // GROUPS
    per = n // GROUPS
    last = steps - 1
    right = ring_row((place + 1) % n, n)
    back = ring_row((place + n - 1) % n, n)

    def aligned(x, m):
        return pl.multiple_of(x, m)

    own_gain = pltpu.make_async_copy(
        gain_in, gain.at[pl.ds(aligned(r * rows, rows), rows), :], gain_sem
    )
    own_gain.start()

    barrier = pltpu.get_barrier_semaphore()

    def greet(i, carry):
        other = ring_row((place + i) % n, n)
        pl.semaphore_signal(barrier, inc=1, device_id=(t, other), device_id_type=MESH)
        return carry

    lax.fori_loop(1, n, greet, 0)

    @pl.when(t > 0)
    def _():
        pl.semaphore_signal(barrier, inc=1, device_id=(t - 1, r), device_id_type=MESH)

    @pl.when(t < last)
    def _():
        pl.semaphore_signal(barrier, inc=1, device_id=(t + 1, r), device_id_type=MESH)

    pl.semaphore_wait(barrier, n - 1 + (t + last - 1) // last + (2 * last - t - 1) // last)

    def cov_copy(source, j):
        columns = pl.ds(aligned(j * part, part), part)
        return pltpu.make_async_remote_copy(
            src_ref=source.at[:, columns],
            dst_ref=cov_next.at[:, columns],
            send_sem=cov_send.at[j],
            recv_sem=cov_recv.at[j],
            device_id=(t - 1, r),
            device_id_type=MESH,
        )

    def mean_copy():
        return pltpu.make_async_remote_copy(
            src_ref=mean_send,
            dst_ref=mean_next,
            send_sem=mean_sems.at[0],
            recv_sem=mean_sems.at[1],
            device_id=(t - 1, r),
            device_id_type=MESH,
        )

    def offset_copy(i):
        other = ring_row((place + i) % n, n)
        return pltpu.make_async_remote_copy(
            src_ref=offset_in,
            dst_ref=offsets.at[r],
            send_sem=offset_send.at[i],
            recv_sem=offset_recv.at[r],
            device_id=(t, other),
            device_id_type=MESH,
        )

    def offset_arrival(i):
        other = ring_row((place + i) % n, n)
        return pltpu.make_async_remote_copy(
            src_ref=offset_in,
            dst_ref=offsets.at[other],
            send_sem=offset_send.at[i],
            recv_sem=offset_recv.at[other],
            device_id=(t, other),
            device_id_type=MESH,
        )

    def ring_copy(way, hop, c):
        origin = ring_row((place + (n - hop if way == 0 else hop)) % n, n)
        span = pl.ds(aligned(origin * rows + way * half + c * piece, piece), piece)
        return pltpu.make_async_remote_copy(
            src_ref=gain.at[span, :],
            dst_ref=gain.at[span, :],
            send_sem=ring_send.at[way, hop, c],
            recv_sem=ring_recv.at[way, hop, c],
            device_id=(t, right if way == 0 else back),
            device_id_type=MESH,
        )

    def ring_arrival(way, hop, c):
        origin = ring_row((place + (n - 1 - hop if way == 0 else hop + 1)) % n, n)
        span = pl.ds(aligned(origin * rows + way * half + c * piece, piece), piece)
        return pltpu.make_async_remote_copy(
            src_ref=gain.at[span, :],
            dst_ref=gain.at[span, :],
            send_sem=ring_send.at[way, hop, c],
            recv_sem=ring_recv.at[way, hop, c],
            device_id=(t, right if way == 0 else back),
            device_id_type=MESH,
        )

    def left_copy(d, way):
        span = pl.ds(way * half, half)
        return pltpu.make_async_remote_copy(
            src_ref=left_out.at[d, span, :],
            dst_ref=left_in.at[r, span, :],
            send_sem=left_send.at[way, d],
            recv_sem=left_recv.at[way, r],
            device_id=(t, d),
            device_id_type=MESH,
        )

    def left_arrival(d, way):
        span = pl.ds(way * half, half)
        return pltpu.make_async_remote_copy(
            src_ref=left_out.at[d, span, :],
            dst_ref=left_in.at[d, span, :],
            send_sem=left_send.at[way, d],
            recv_sem=left_recv.at[way, d],
            device_id=(t, d),
            device_id_type=MESH,
        )

    def await_cov():
        for j in range(GROUPS):
            cov_copy(cov_in, j).wait_recv()

    @pl.when(t == last)
    def _():
        for j in range(GROUPS):
            cov_copy(cov_in, j).start()

    def send_offset(i, carry):
        offset_copy(i).start()
        return carry

    lax.fori_loop(1, n, send_offset, 0)
    own_gain.wait()

    def left_half(d, way):
        block = gain[pl.ds(aligned(d * rows + way * half, half), half), :]
        product = lax.dot_general(
            block, cov_next[...], CONTRACT_LAST, preferred_element_type=jnp.float32
        )
        return product.astype(jnp.bfloat16)

    @pl.when(t < last)
    def _():
        @pl.when(t % 2 == 0)
        def _():
            @pl.when(t < last - 1)
            def _():
                pl.semaphore_wait(gate, 1)

        for c in range(CHUNKS):
            for way in range(2):
                ring_copy(way, 0, c).start()

        @pl.when(t == last - 1)
        def _():
            await_cov()
            for way in range(2):
                left_in[r, pl.ds(way * half, half), :] = left_half(r, way)

        def pass_on(hop, carry):
            for c in range(CHUNKS):
                for way in range(2):
                    ring_arrival(way, hop - 1, c).wait_recv()
                    ring_copy(way, hop, c).start()

            @pl.when(t == last - 1)
            def _():
                for way in range(2):
                    d = ring_row((place + (n - hop if way == 0 else hop)) % n, n)
                    left_out[d, pl.ds(way * half, half), :] = left_half(d, way)
                    left_copy(d, way).start()

            return carry

        lax.fori_loop(1, n - 1, pass_on, 0)

        for c in range(CHUNKS):
            for way in range(2):
                ring_arrival(way, n - 2, c).wait_recv()

        @pl.when(t % 2 == 1)
        def _():
            pl.semaphore_signal(gate, inc=1, device_id=(t - 1, r), device_id_type=MESH)

        @pl.when(t == last - 1)
        def _():
            for way in range(2):
                d = ring_row((place + (1 if way == 0 else n - 1)) % n, n)
                left_out[d, pl.ds(way * half, half), :] = left_half(d, way)
                left_copy(d, way).start()

    offsets[r] = offset_in[...]

    def await_offset(i, carry):
        offset_arrival(i).wait_recv()
        return carry

    lax.fori_loop(1, n, await_offset, 0)
    whole_offset = offsets[0]
    for i in range(1, n):
        whole_offset = whole_offset + offsets[i]

    @pl.when(t == last)
    def _():
        mean_send[...] = whole_offset
        mean_copy().start()
        mean_out[...] = whole_offset
        cov_out[...] = cov_in[...]

    @pl.when(t < last)
    def _():
        @pl.when(t < last - 1)
        def _():
            await_cov()

            def left_part(j, carry):
                g = (r // per + 1 + j) % GROUPS
                block = gain[pl.ds(aligned(g * part, part), part), :]
                product = lax.dot_general(
                    block, cov_next[...], CONTRACT_LAST, preferred_element_type=jnp.float32
                ).astype(jnp.bfloat16)
                for i in range(per):
                    d = g * per + i
                    left_out[d] = product[i * rows:(i + 1) * rows]

                    @pl.when(d != r)
                    def _():
                        for way in range(2):
                            left_copy(d, way).start()

                    @pl.when(d == r)
                    def _():
                        left_in[r] = product[i * rows:(i + 1) * rows]

                return carry

            lax.fori_loop(0, GROUPS, left_part, 0)

        mean_copy().wait_recv()
        left[rows:, :] = jnp.broadcast_to(mean_next[...], (PAD, size)).astype(jnp.bfloat16)

        def await_left(i, carry):
            for way in range(2):
                left_arrival(ring_row((place + i) % n, n), way).wait_recv()
            return carry

        lax.fori_loop(1, n, await_left, 0)
        for d in range(n):
            left[0:rows, d * rows:(d + 1) * rows] = left_in[d]

        offsets[0] = whole_offset

        def right_part(j, carry):
            columns = pl.ds(aligned(j * part, part), part)
            product = lax.dot_general(
                left[...], gain[columns, :], CONTRACT_LAST, preferred_element_type=jnp.float32
            )
            cov_out[:, columns] = (
                product[:rows] + cov_in[:, columns].astype(jnp.float32)
            ).astype(jnp.bfloat16)
            mean = product[rows:rows + 1] + offsets[0, :, columns]
            mean_send[:, columns] = mean.astype(jnp.bfloat16).astype(jnp.float32)

            @pl.when(t > 0)
            def _():
                cov_copy(cov_out, j).start()

            return carry

        lax.fori_loop(0, GROUPS, right_part, 0)
        mean_out[...] = mean_send[...]

        @pl.when(t > 0)
        def _():
            mean_copy().start()

        def left_gone(i, carry):
            for way in range(2):
                left_copy(ring_row((place + i) % n, n), way).wait_send()
            return carry

        lax.fori_loop(1, n, left_gone, 0)

        def ring_gone(hop, carry):
            for c in range(CHUNKS):
                for way in range(2):
                    ring_copy(way, hop, c).wait_send()
            return carry

        lax.fori_loop(0, n - 1, ring_gone, 0)

    @pl.when(t > 0)
    def _():
        for j in range(GROUPS):
            cov_copy(cov_out, j).wait_send()
        mean_copy().wait_send()

    def offset_gone(i, carry):
        offset_copy(i).wait_send()
        return carry

    lax.fori_loop(1, n, offset_gone, 0)


def shards(steps, n, smoother_gains, smoother_offsets, smoother_covs):
    own_gain = smoother_gains[0]
    own_cov = smoother_covs[0]
    rows, size = own_cov.shape
    start = lax.axis_index("rows") * rows
    offset_row = lax.dynamic_update_slice(
        jnp.zeros((1, size), jnp.float32), smoother_offsets.astype(jnp.float32), (0, start)
    )
    vmem = pl.BlockSpec(memory_space=pltpu.VMEM)
    dma = pltpu.SemaphoreType.DMA
    mean_row, cov = pl.pallas_call(
        functools.partial(kernel, steps, n),
        out_shape=(
            jax.ShapeDtypeStruct((1, size), jnp.float32),
            jax.ShapeDtypeStruct((rows, size), jnp.bfloat16),
        ),
        in_specs=[pl.BlockSpec(memory_space=pl.ANY), vmem, vmem],
        out_specs=(vmem, vmem),
        scratch_shapes=[
            pltpu.VMEM((size, size), jnp.bfloat16),
            pltpu.VMEM((rows, size), jnp.bfloat16),
            pltpu.VMEM((n, rows, rows), jnp.bfloat16),
            pltpu.VMEM((n, rows, rows), jnp.bfloat16),
            pltpu.VMEM((rows + PAD, size), jnp.bfloat16),
            pltpu.VMEM((n, 1, size), jnp.float32),
            pltpu.VMEM((1, size), jnp.float32),
            pltpu.VMEM((1, size), jnp.float32),
            dma,
            dma((2, n, CHUNKS)),
            dma((2, n, CHUNKS)),
            dma((2, n)),
            dma((2, n)),
            dma((n,)),
            dma((n,)),
            dma((GROUPS,)),
            dma((GROUPS,)),
            dma((2,)),
            pltpu.SemaphoreType.REGULAR,
        ],
        compiler_params=pltpu.CompilerParams(
            collective_id=0, has_side_effects=True, vmem_limit_bytes=40 << 20
        ),
    )(own_gain, offset_row, own_cov)
    mean = lax.dynamic_slice(mean_row, (0, start), (1, rows)).astype(jnp.bfloat16)
    return mean, cov[None]


def solution(mesh):
    in_specs = (P("tm", "rows", None), P("tm", "rows"), P("tm", "rows", None))
    out_specs = (P("tm", "rows"), P("tm", "rows", None))
    body = functools.partial(shards, mesh.shape["tm"], mesh.shape["rows"])
    return jax.shard_map(body, mesh=mesh, in_specs=in_specs, out_specs=out_specs, check_vma=False)
```

time: 384 us -> 87.4 us (0.23)
  waiting for transfers between devices: 275 us -> 0 us
  Pallas kernels: 0 us -> 81.5 us
  blocking collectives: 56.6 us -> 0 us
  matrix products: 25.7 us -> 0 us
  between operations: 14.5 us -> 0.67 us
  starting transfers between devices: 7.96 us -> 0 us
    all_gather x4 -> x0, waiting for transfers between devices: 256 us -> none  [the longest x3 176 us: shards(): lax.all_gather(cov_in, 'rows', axis=0, tiled=True)]
    pallas_call x0 -> x1, Pallas kernels: none -> 81.5 us  [shards(): pl.pallas_call(functools.partial(kernel, steps, n), out_shape=(jax.ShapeD...]
    unnamed x3 -> x0, blocking collectives: 56.6 us -> none
    dot_general x6 -> x0, matrix products: 25.7 us -> none  [the longest x3 25 us: shards(): lax.dot_general(left_times.astype(jnp.bfloat16), whole_gain, (((1,), (1,)...]
    ppermute x6 -> x0, waiting for transfers between devices: 18.6 us -> none  [from_behind(): return lax.ppermute(block, axis, route)]
    ppermute x6 -> x0, starting transfers between devices: 7.8 us -> none  [from_behind(): return lax.ppermute(block, axis, route)]
  transfers between devices with their start and end apart: 10 -> 0, of which waited for: 10 -> 0; matrix products, arithmetic and copies ran while one was open for 1% -> 0% of each run, Pallas kernels for 0% -> 0%
where the time goes in v1:
time: 87.4 us; the launch traced here: 86.6 us
  Pallas kernels  81.5 us (93%)
  local copies, waits for them, and re-layouts  4.4 us (5%)
    pallas_call x1, Pallas kernels, shards(): pl.pallas_call(functools.partial(kernel, steps, n), out_shape=(jax.ShapeD...  81.5 us
    unnamed x7, local copies, waits for them, and re-layouts  3.61 us

profile of v1, /device:TPU:0, one launch (start us, length us, event | category | flops | bytes accessed | tf_op | source)
XLA Modules:
  0.0 86.6 jit_solution(13228524864588163129)
XLA Ops:
  0.6 0.0 copy-start.2
  0.6 0.7 copy-done.2
  1.3 0.1 dynamic_update_slice.3.offset_in
  1.5 0.0 copy-start
  1.5 1.1 %copy-done = bf16[1,192,1536]{2,1,0:T(8,128)(2,1)S(1)} copy-done((bf16[1,192,1536]{2,1,0:T(8,128)(2,1)S(1)}, bf16[1,192,1536]{2,1,0:T(8,128)(2,1)}, u32[]{:S(2)}) %copy-start) | copy-done | bytes 589848
  2.5 0.0 copy-start.1
  2.5 1.1 %copy-done.1 = bf16[1,192,1536]{2,1,0:T(8,128)(2,1)S(1)} copy-done((bf16[1,192,1536]{2,1,0:T(8,128)(2,1)S(1)}, bf16[1,192,1536]{2,1,0:T(8,128)(2,1)}, u32[]{:S(2)}) %copy-start.1) | copy-done | bytes 589848
  3.6 81.5 %shard_map.50 = (f32[1,1536]{1,0:T(1,128)S(1)}, bf16[192,1536]{1,0:T(8,128)(2,1)S(1)}) custom-call(bf16[192,1536]{1,0:T(8,128)(2,1)S(1)} %bitcast.3, f32[1,1536]{1,0:T(1,128)S(1)} %dynamic_update_slice.3.offset_in, bf16[192,1536]{1,0:T(8,128)(2,1)S(1)} %bitcast.4), custom_call_target="tpu_custom_call" | custom-call | tf_op jit(solution)/shard_map/pallas_call | solution.py:357
  85.1 0.6 dynamic-slice_convert_fusion
  85.8 0.8 copy.7
  (2 shorter events, 0.0 us)
Async XLA Ops:
  0.6 0.7 copy-start.2
  1.5 1.1 %copy-start = (bf16[1,192,1536]{2,1,0:T(8,128)(2,1)S(1)}, bf16[1,192,1536]{2,1,0:T(8,128)(2,1)}, u32[]{:S(2)}) copy-start(bf16[1,192,1536]{2,1,0:T(8,128)(2,1)} %param.3) | copy-start | bytes 1769476
  2.5 1.1 %copy-start.1 = (bf16[1,192,1536]{2,1,0:T(8,128)(2,1)S(1)}, bf16[1,192,1536]{2,1,0:T(8,128)(2,1)}, u32[]{:S(2)}) copy-start(bf16[1,192,1536]{2,1,0:T(8,128)(2,1)} %param.5) | copy-start | bytes 1769476

commit v2 on v1

--- a/solution.py
+++ b/solution.py
@@ -10,6 +10,8 @@
 MESH = pl.DeviceIdType.MESH
 CHUNKS = 3
 GROUPS = 4
+LEFT_GROUPS = 2
+HEAD_START = 2
 PAD = 16
 CONTRACT_LAST = (((1,), (1,)), ((), ()))
 
@@ -24,11 +26,15 @@
     return (1 - odd) * (row // 2) + odd * (n - 1 - row // 2)
 
 
+def main_lanes(rows):
+    return 128 if rows == 192 else rows
+
+
 def kernel(
-    steps, n, gain_in, offset_in, cov_in, mean_out, cov_out,
-    gain, cov_next, left_out, left_in, left, offsets, mean_next, mean_send,
+    steps, n, gain_in, offset_in, cov_hbm, mean_out, cov_hbm_out,
+    gain, cov_in, cov_out, cov_next, left_out, left_in, left, offsets, mean_next, mean_send,
     gain_sem, ring_send, ring_recv, left_send, left_recv,
-    offset_send, offset_recv, cov_send, cov_recv, mean_sems, gate,
+    offset_send, offset_recv, cov_send, cov_recv, mean_sems, cov_sem, out_sem, gate,
 ):
     t = lax.axis_index("tm")
     r = lax.axis_index("rows")
@@ -37,7 +43,8 @@
     half = rows // 2
     piece = half // CHUNKS
     part = size // GROUPS
-    per = n // GROUPS
+    left_part_rows = size // LEFT_GROUPS
+    per = n // LEFT_GROUPS
     last = steps - 1
     right = ring_row((place + 1) % n, n)
     back = ring_row((place + n - 1) % n, n)
@@ -49,6 +56,33 @@
         gain_in, gain.at[pl.ds(aligned(r * rows, rows), rows), :], gain_sem
     )
     own_gain.start()
+    own_cov = pltpu.make_async_copy(cov_hbm, cov_in, cov_sem)
+    own_cov.start()
+
+    def store_cov(j):
+        columns = pl.ds(aligned(j * part, part), part)
+        return pltpu.make_async_copy(
+            cov_out.at[:, columns], cov_hbm_out.at[:, columns], out_sem.at[j]
+        )
+
+    def store_block(ref, index, way, block):
+        main = main_lanes(rows)
+        ref[index, way, 0:half, :] = block[:, :main]
+        if main < rows:
+            for i in range(2):
+                ref[index, way, half:, i * 64:(i + 1) * 64] = block[
+                    i * half // 2:(i + 1) * half // 2, main:
+                ]
+
+    def place_block(d, way):
+        main = main_lanes(rows)
+        top, at = way * half, d * rows
+        left[top:top + half, at:at + main] = left_in[d, way, 0:half, :]
+        if main < rows:
+            for i in range(2):
+                left[top + i * half // 2:top + (i + 1) * half // 2, at + main:at + rows] = (
+                    left_in[d, way, half:, i * 64:(i + 1) * 64]
+                )
 
     barrier = pltpu.get_barrier_semaphore()
 
@@ -137,10 +171,9 @@
         )
 
     def left_copy(d, way):
-        span = pl.ds(way * half, half)
-        return pltpu.make_async_remote_copy(
-            src_ref=left_out.at[d, span, :],
-            dst_ref=left_in.at[r, span, :],
+        return pltpu.make_async_remote_copy(
+            src_ref=left_out.at[d, way],
+            dst_ref=left_in.at[r, way],
             send_sem=left_send.at[way, d],
             recv_sem=left_recv.at[way, r],
             device_id=(t, d),
@@ -148,10 +181,9 @@
         )
 
     def left_arrival(d, way):
-        span = pl.ds(way * half, half)
-        return pltpu.make_async_remote_copy(
-            src_ref=left_out.at[d, span, :],
-            dst_ref=left_in.at[d, span, :],
+        return pltpu.make_async_remote_copy(
+            src_ref=left_out.at[d, way],
+            dst_ref=left_in.at[d, way],
             send_sem=left_send.at[way, d],
             recv_sem=left_recv.at[way, d],
             device_id=(t, d),
@@ -161,6 +193,8 @@
     def await_cov():
         for j in range(GROUPS):
             cov_copy(cov_in, j).wait_recv()
+
+    own_cov.wait()
 
     @pl.when(t == last)
     def _():
@@ -197,7 +231,7 @@
         def _():
             await_cov()
             for way in range(2):
-                left_in[r, pl.ds(way * half, half), :] = left_half(r, way)
+                store_block(left_in, r, way, left_half(r, way))
 
         def pass_on(hop, carry):
             for c in range(CHUNKS):
@@ -205,11 +239,17 @@
                     ring_arrival(way, hop - 1, c).wait_recv()
                     ring_copy(way, hop, c).start()
 
+            @pl.when(hop == min(HEAD_START, n - 2))
+            def _():
+                @pl.when(t % 2 == 1)
+                def _():
+                    pl.semaphore_signal(gate, inc=1, device_id=(t - 1, r), device_id_type=MESH)
+
             @pl.when(t == last - 1)
             def _():
                 for way in range(2):
                     d = ring_row((place + (n - hop if way == 0 else hop)) % n, n)
-                    left_out[d, pl.ds(way * half, half), :] = left_half(d, way)
+                    store_block(left_out, d, way, left_half(d, way))
                     left_copy(d, way).start()
 
             return carry
@@ -219,16 +259,12 @@
         for c in range(CHUNKS):
             for way in range(2):
                 ring_arrival(way, n - 2, c).wait_recv()
-
-        @pl.when(t % 2 == 1)
-        def _():
-            pl.semaphore_signal(gate, inc=1, device_id=(t - 1, r), device_id_type=MESH)
 
         @pl.when(t == last - 1)
         def _():
             for way in range(2):
                 d = ring_row((place + (1 if way == 0 else n - 1)) % n, n)
-                left_out[d, pl.ds(way * half, half), :] = left_half(d, way)
+                store_block(left_out, d, way, left_half(d, way))
                 left_copy(d, way).start()
 
     offsets[r] = offset_in[...]
@@ -247,7 +283,9 @@
         mean_send[...] = whole_offset
         mean_copy().start()
         mean_out[...] = whole_offset
-        cov_out[...] = cov_in[...]
+        keep = pltpu.make_async_copy(cov_in, cov_hbm_out, cov_sem)
+        keep.start()
+        keep.wait()
 
     @pl.when(t < last)
     def _():
@@ -256,27 +294,33 @@
             await_cov()
 
             def left_part(j, carry):
-                g = (r // per + 1 + j) % GROUPS
-                block = gain[pl.ds(aligned(g * part, part), part), :]
+                g = (r // per + 1 + j) % LEFT_GROUPS
+                span = pl.ds(aligned(g * left_part_rows, left_part_rows), left_part_rows)
                 product = lax.dot_general(
-                    block, cov_next[...], CONTRACT_LAST, preferred_element_type=jnp.float32
+                    gain[span, :], cov_next[...], CONTRACT_LAST,
+                    preferred_element_type=jnp.float32,
                 ).astype(jnp.bfloat16)
                 for i in range(per):
                     d = g * per + i
-                    left_out[d] = product[i * rows:(i + 1) * rows]
+                    for way in range(2):
+                        top = i * rows + way * half
+                        store_block(left_out, d, way, product[top:top + half])
+
+                def send(i, carry):
+                    d = g * per + (r + i) % per
 
                     @pl.when(d != r)
                     def _():
                         for way in range(2):
                             left_copy(d, way).start()
 
-                    @pl.when(d == r)
-                    def _():
-                        left_in[r] = product[i * rows:(i + 1) * rows]
-
+                    return carry
+
+                lax.fori_loop(0, per, send, 0)
                 return carry
 
-            lax.fori_loop(0, GROUPS, left_part, 0)
+            lax.fori_loop(0, LEFT_GROUPS, left_part, 0)
+            left_in[r] = left_out[r]
 
         mean_copy().wait_recv()
         left[rows:, :] = jnp.broadcast_to(mean_next[...], (PAD, size)).astype(jnp.bfloat16)
@@ -288,7 +332,8 @@
 
         lax.fori_loop(1, n, await_left, 0)
         for d in range(n):
-            left[0:rows, d * rows:(d + 1) * rows] = left_in[d]
+            for way in range(2):
+                place_block(d, way)
 
         offsets[0] = whole_offset
 
@@ -307,6 +352,7 @@
             def _():
                 cov_copy(cov_out, j).start()
 
+            store_cov(j).start()
             return carry
 
         lax.fori_loop(0, GROUPS, right_part, 0)
@@ -315,6 +361,9 @@
         @pl.when(t > 0)
         def _():
             mean_copy().start()
+
+        for j in range(GROUPS):
+            store_cov(j).wait()
 
         def left_gone(i, carry):
             for way in range(2):
@@ -353,6 +402,9 @@
         jnp.zeros((1, size), jnp.float32), smoother_offsets.astype(jnp.float32), (0, start)
     )
     vmem = pl.BlockSpec(memory_space=pltpu.VMEM)
+    hbm = pl.BlockSpec(memory_space=pl.ANY)
+    lanes = main_lanes(rows)
+    folded = (n, 2, rows // 2 * rows // lanes, lanes)
     dma = pltpu.SemaphoreType.DMA
     mean_row, cov = pl.pallas_call(
         functools.partial(kernel, steps, n),
@@ -360,13 +412,15 @@
             jax.ShapeDtypeStruct((1, size), jnp.float32),
             jax.ShapeDtypeStruct((rows, size), jnp.bfloat16),
         ),
-        in_specs=[pl.BlockSpec(memory_space=pl.ANY), vmem, vmem],
-        out_specs=(vmem, vmem),
+        in_specs=[hbm, vmem, hbm],
+        out_specs=(vmem, hbm),
         scratch_shapes=[
             pltpu.VMEM((size, size), jnp.bfloat16),
             pltpu.VMEM((rows, size), jnp.bfloat16),
-            pltpu.VMEM((n, rows, rows), jnp.bfloat16),
-            pltpu.VMEM((n, rows, rows), jnp.bfloat16),
+            pltpu.VMEM((rows, size), jnp.bfloat16),
+            pltpu.VMEM((rows, size), jnp.bfloat16),
+            pltpu.VMEM(folded, jnp.bfloat16),
+            pltpu.VMEM(folded, jnp.bfloat16),
             pltpu.VMEM((rows + PAD, size), jnp.bfloat16),
             pltpu.VMEM((n, 1, size), jnp.float32),
             pltpu.VMEM((1, size), jnp.float32),
@@ -381,10 +435,12 @@
             dma((GROUPS,)),
             dma((GROUPS,)),
             dma((2,)),
+            dma,
+            dma((GROUPS,)),
             pltpu.SemaphoreType.REGULAR,
         ],
         compiler_params=pltpu.CompilerParams(
-            collective_id=0, has_side_effects=True, vmem_limit_bytes=40 << 20
+            collective_id=0, has_side_effects=True, vmem_limit_bytes=62 << 20
         ),
     )(own_gain, offset_row, own_cov)
     mean = lax.dynamic_slice(mean_row, (0, start), (1, rows)).astype(jnp.bfloat16)

time: 87.4 us -> 86 us (0.984)
  Pallas kernels: 81.5 us -> 80.4 us
    pallas_call x1, Pallas kernels: 81.5 us -> 80.4 us  [shards(): pl.pallas_call(functools.partial(kernel, steps, n), out_shape=(jax.ShapeD...]
    unnamed x7 -> x5, local copies, waits for them, and re-layouts: 3.61 us -> 3.18 us
where the time goes in v2:
time: 86 us; the launch traced here: 85.7 us
  Pallas kernels  80.4 us (93%)
  local copies, waits for them, and re-layouts  4.64 us (5%)
    pallas_call x1, Pallas kernels, shards(): pl.pallas_call(functools.partial(kernel, steps, n), out_shape=(jax.ShapeD...  80.4 us
    unnamed x5, local copies, waits for them, and re-layouts  3.18 us

profile of v2, /device:TPU:0, one launch (start us, length us, event | category | flops | bytes accessed | tf_op | source)
XLA Modules:
  0.0 85.7 jit_solution(10658498040952627023)
XLA Ops:
  0.6 0.0 copy-start.1
  0.6 0.7 copy-done.1
  1.3 0.1 dynamic_update_slice.3.offset_in
  1.5 0.0 copy-start
  1.5 0.6 copy-done
  2.1 80.4 %shard_map.50 = (f32[1,1536]{1,0:T(1,128)}, bf16[192,1536]{1,0:T(8,128)(2,1)}) custom-call(bf16[192,1536]{1,0:T(8,128)(2,1)} %bitcast.3, f32[1,1536]{1,0:T(1,128)} %copy-done, bf16[192,1536]{1,0:T(8,128)(2,1)} %bitcast.4), custom_call_target="tpu_custom_call" | custom-call | tf_op jit(solution)/shard_map/pallas_call | solution.py:409
  82.5 1.3 %dynamic-slice_convert_fusion = bf16[1,192]{1,0:T(2,128)(2,1)} fusion(f32[1,1536]{1,0:T(1,128)} %get-tuple-element.4, s32[]{:T(128)S(6)} %select_n.4), kind=kLoop, calls=%fused_computation | loop fusion | bytes 772 | tf_op jit(solution)/shard_map/convert_element_type | solution.py:446
  83.8 1.9 %copy.7 = bf16[1,192,1536]{2,1,0:T(8,128)(2,1)} copy(bf16[1,192,1536]{2,1,0:T(8,128)(2,1)} %bitcast.5) | data formatting | bytes 1179648
  (2 shorter events, 0.0 us)
Async XLA Ops:
  0.6 0.7 copy-start.1
  1.5 0.6 copy-start

commit v3 on v2

--- a/solution.py
+++ b/solution.py
@@ -8,10 +8,11 @@
 from jax.sharding import PartitionSpec as P
 
 MESH = pl.DeviceIdType.MESH
-CHUNKS = 3
+PIECES = 6
+THIRDS = 3
 GROUPS = 4
 LEFT_GROUPS = 2
-HEAD_START = 2
+HEAD_START = 4
 PAD = 16
 CONTRACT_LAST = (((1,), (1,)), ((), ()))
 
@@ -34,18 +35,21 @@
     steps, n, gain_in, offset_in, cov_hbm, mean_out, cov_hbm_out,
     gain, cov_in, cov_out, cov_next, left_out, left_in, left, offsets, mean_next, mean_send,
     gain_sem, ring_send, ring_recv, left_send, left_recv,
-    offset_send, offset_recv, cov_send, cov_recv, mean_sems, cov_sem, out_sem, gate,
+    offset_send, offset_recv, cov_send, cov_recv, mean_sems, cov_sem, out_sem,
+    relay, seed_send, seed_recv, relay_send, relay_recv, back_send, back_recv, gate,
 ):
     t = lax.axis_index("tm")
     r = lax.axis_index("rows")
     place = ring_place(r, n)
     rows, size = cov_in.shape
-    half = rows // 2
-    piece = half // CHUNKS
+    third = rows // THIRDS
+    piece = rows // PIECES
     part = size // GROUPS
     left_part_rows = size // LEFT_GROUPS
     per = n // LEFT_GROUPS
     last = steps - 1
+    first = last - 1
+    helper = last - 3
     right = ring_row((place + 1) % n, n)
     back = ring_row((place + n - 1) % n, n)
 
@@ -53,7 +57,7 @@
         return pl.multiple_of(x, m)
 
     own_gain = pltpu.make_async_copy(
-        gain_in, gain.at[pl.ds(aligned(r * rows, rows), rows), :], gain_sem
+        gain_in, gain.at[r], gain_sem
     )
     own_gain.start()
     own_cov = pltpu.make_async_copy(cov_hbm, cov_in, cov_sem)
@@ -67,21 +71,21 @@
 
     def store_block(ref, index, way, block):
         main = main_lanes(rows)
-        ref[index, way, 0:half, :] = block[:, :main]
+        ref[index, way, 0:third, :] = block[:, :main]
         if main < rows:
             for i in range(2):
-                ref[index, way, half:, i * 64:(i + 1) * 64] = block[
-                    i * half // 2:(i + 1) * half // 2, main:
+                ref[index, way, third:, i * 64:(i + 1) * 64] = block[
+                    i * third // 2:(i + 1) * third // 2, main:
                 ]
 
     def place_block(d, way):
         main = main_lanes(rows)
-        top, at = way * half, d * rows
-        left[top:top + half, at:at + main] = left_in[d, way, 0:half, :]
+        top, at = way * third, d * rows
+        left[top:top + third, at:at + main] = left_in[d, way, 0:third, :]
         if main < rows:
             for i in range(2):
-                left[top + i * half // 2:top + (i + 1) * half // 2, at + main:at + rows] = (
-                    left_in[d, way, half:, i * 64:(i + 1) * 64]
+                left[top + i * third // 2:top + (i + 1) * third // 2, at + main:at + rows] = (
+                    left_in[d, way, third:, i * 64:(i + 1) * 64]
                 )
 
     barrier = pltpu.get_barrier_semaphore()
@@ -101,7 +105,20 @@
     def _():
         pl.semaphore_signal(barrier, inc=1, device_id=(t + 1, r), device_id_type=MESH)
 
-    pl.semaphore_wait(barrier, n - 1 + (t + last - 1) // last + (2 * last - t - 1) // last)
+    @pl.when(t == first)
+    def _():
+        pl.semaphore_signal(barrier, inc=1, device_id=(helper, r), device_id_type=MESH)
+
+    @pl.when(t == helper)
+    def _():
+        pl.semaphore_signal(barrier, inc=1, device_id=(first, r), device_id_type=MESH)
+
+    def same(x, y):
+        square = steps * steps
+        return 1 - ((x - y) * (x - y) + square - 1) // square
+
+    greetings = n + 1 - same(t, 0) - same(t, last) + same(t, first) + same(t, helper)
+    pl.semaphore_wait(barrier, greetings)
 
     def cov_copy(source, j):
         columns = pl.ds(aligned(j * part, part), part)
@@ -146,27 +163,60 @@
             device_id_type=MESH,
         )
 
-    def ring_copy(way, hop, c):
-        origin = ring_row((place + (n - hop if way == 0 else hop)) % n, n)
-        span = pl.ds(aligned(origin * rows + way * half + c * piece, piece), piece)
-        return pltpu.make_async_remote_copy(
-            src_ref=gain.at[span, :],
-            dst_ref=gain.at[span, :],
+    def sent_origin(way, hop):
+        return ring_row((place + (n - hop if way == 0 else hop)) % n, n)
+
+    def ring_part(origin, way, hop, c, chunks):
+        span = pl.ds((way * chunks + c) * piece, piece)
+        return pltpu.make_async_remote_copy(
+            src_ref=gain.at[origin, span, :],
+            dst_ref=gain.at[origin, span, :],
             send_sem=ring_send.at[way, hop, c],
             recv_sem=ring_recv.at[way, hop, c],
             device_id=(t, right if way == 0 else back),
             device_id_type=MESH,
         )
 
-    def ring_arrival(way, hop, c):
-        origin = ring_row((place + (n - 1 - hop if way == 0 else hop + 1)) % n, n)
-        span = pl.ds(aligned(origin * rows + way * half + c * piece, piece), piece)
-        return pltpu.make_async_remote_copy(
-            src_ref=gain.at[span, :],
-            dst_ref=gain.at[span, :],
-            send_sem=ring_send.at[way, hop, c],
-            recv_sem=ring_recv.at[way, hop, c],
+    def ring_copy(way, hop, c, chunks):
+        return ring_part(sent_origin(way, hop), way, hop, c, chunks)
+
+    def ring_arrival(way, hop, c, chunks):
+        return ring_part(sent_origin(way, hop + 1), way, hop, c, chunks)
+
+    def seed_copy(way):
+        return pltpu.make_async_remote_copy(
+            src_ref=gain.at[r, pl.ds((4 + way) * piece, piece), :],
+            dst_ref=relay.at[r, way],
+            send_sem=seed_send.at[way],
+            recv_sem=seed_recv.at[way],
+            device_id=(helper, r),
+            device_id_type=MESH,
+        )
+
+    def relay_part(origin, way, hop):
+        return pltpu.make_async_remote_copy(
+            src_ref=relay.at[origin, way],
+            dst_ref=relay.at[origin, way],
+            send_sem=relay_send.at[way, hop],
+            recv_sem=relay_recv.at[way, hop],
             device_id=(t, right if way == 0 else back),
+            device_id_type=MESH,
+        )
+
+    def relay_copy(way, hop):
+        return relay_part(sent_origin(way, hop), way, hop)
+
+    def relay_arrival(way, hop):
+        return relay_part(sent_origin(way, hop + 1), way, hop)
+
+    def back_copy(way, hop):
+        origin = sent_origin(way, hop + 1)
+        return pltpu.make_async_remote_copy(
+            src_ref=relay.at[origin, way],
+            dst_ref=gain.at[origin, pl.ds((4 + way) * piece, piece), :],
+            send_sem=back_send.at[way, hop],
+            recv_sem=back_recv.at[way, hop],
+            device_id=(first, r),
             device_id_type=MESH,
         )
 
@@ -208,64 +258,131 @@
     lax.fori_loop(1, n, send_offset, 0)
     own_gain.wait()
 
-    def left_half(d, way):
-        block = gain[pl.ds(aligned(d * rows + way * half, half), half), :]
+    def left_third(d, way):
         product = lax.dot_general(
-            block, cov_next[...], CONTRACT_LAST, preferred_element_type=jnp.float32
+            gain[d, pl.ds(way * third, third), :], cov_next[...], CONTRACT_LAST,
+            preferred_element_type=jnp.float32,
         )
         return product.astype(jnp.bfloat16)
 
-    @pl.when(t < last)
+    def send_third(d, way):
+        store_block(left_out, d, way, left_third(d, way))
+        left_copy(d, way).start()
+
+    def go_round(chunks, begin, between):
+        for c in range(chunks):
+            for way in range(2):
+                ring_copy(way, 0, c, chunks).start()
+        begin()
+
+        def pass_on(hop, carry):
+            for c in range(chunks):
+                for way in range(2):
+                    ring_arrival(way, hop - 1, c, chunks).wait_recv()
+                    ring_copy(way, hop, c, chunks).start()
+            between(hop)
+            return carry
+
+        lax.fori_loop(1, n - 1, pass_on, 0)
+        for c in range(chunks):
+            for way in range(2):
+                ring_arrival(way, n - 2, c, chunks).wait_recv()
+
+    def round_gone(chunks):
+        def gone(hop, carry):
+            for c in range(chunks):
+                for way in range(2):
+                    ring_copy(way, hop, c, chunks).wait_send()
+            return carry
+
+        lax.fori_loop(0, n - 1, gone, 0)
+
+    @pl.when(t == first)
+    def _():
+        for way in range(2):
+            seed_copy(way).start()
+
+        def begin():
+            await_cov()
+            for way in range(THIRDS):
+                store_block(left_in, r, way, left_third(r, way))
+
+        def between(hop):
+            for way in range(2):
+                send_third(sent_origin(way, hop), way)
+
+        go_round(2, begin, between)
+        for way in range(2):
+            send_third(sent_origin(way, n - 1), way)
+
+        def returned(hop, carry):
+            for way in range(2):
+                back_copy(way, hop).wait_recv()
+            return carry
+
+        lax.fori_loop(0, n - 1, returned, 0)
+        tail = gain[:, 2 * third:, :].reshape(n * third, size)
+        product = lax.dot_general(
+            tail, cov_next[...], CONTRACT_LAST, preferred_element_type=jnp.float32
+        ).astype(jnp.bfloat16)
+        for d in range(n):
+            store_block(left_out, d, 2, product[d * third:(d + 1) * third])
+
+        def send_tail(i, carry):
+            left_copy(ring_row((place + i) % n, n), 2).start()
+            return carry
+
+        lax.fori_loop(1, n, send_tail, 0)
+        round_gone(2)
+        for way in range(2):
+            seed_copy(way).wait_send()
+
+    @pl.when(t == helper)
+    def _():
+        for way in range(2):
+            seed_copy(way).wait_recv()
+            relay_copy(way, 0).start()
+
+        def relay_on(hop, carry):
+            for way in range(2):
+                relay_arrival(way, hop - 1).wait_recv()
+                relay_copy(way, hop).start()
+                back_copy(way, hop - 1).start()
+            return carry
+
+        lax.fori_loop(1, n - 1, relay_on, 0)
+        for way in range(2):
+            relay_arrival(way, n - 2).wait_recv()
+            back_copy(way, n - 2).start()
+
+    @pl.when(t < first)
     def _():
         @pl.when(t % 2 == 0)
         def _():
-            @pl.when(t < last - 1)
-            def _():
-                pl.semaphore_wait(gate, 1)
-
-        for c in range(CHUNKS):
-            for way in range(2):
-                ring_copy(way, 0, c).start()
-
-        @pl.when(t == last - 1)
-        def _():
-            await_cov()
-            for way in range(2):
-                store_block(left_in, r, way, left_half(r, way))
-
-        def pass_on(hop, carry):
-            for c in range(CHUNKS):
-                for way in range(2):
-                    ring_arrival(way, hop - 1, c).wait_recv()
-                    ring_copy(way, hop, c).start()
-
+            pl.semaphore_wait(gate, 1)
+
+        def begin():
+            pass
+
+        def between(hop):
             @pl.when(hop == min(HEAD_START, n - 2))
             def _():
                 @pl.when(t % 2 == 1)
                 def _():
                     pl.semaphore_signal(gate, inc=1, device_id=(t - 1, r), device_id_type=MESH)
 
-            @pl.when(t == last - 1)
-            def _():
-                for way in range(2):
-                    d = ring_row((place + (n - hop if way == 0 else hop)) % n, n)
-                    store_block(left_out, d, way, left_half(d, way))
-                    left_copy(d, way).start()
-
-            return carry
-
-        lax.fori_loop(1, n - 1, pass_on, 0)
-
-        for c in range(CHUNKS):
+        go_round(3, begin, between)
+        round_gone(3)
+
+    @pl.when(t == helper)
+    def _():
+        def relayed(hop, carry):
             for way in range(2):
-                ring_arrival(way, n - 2, c).wait_recv()
-
-        @pl.when(t == last - 1)
-        def _():
-            for way in range(2):
-                d = ring_row((place + (1 if way == 0 else n - 1)) % n, n)
-                store_block(left_out, d, way, left_half(d, way))
-                left_copy(d, way).start()
+                relay_copy(way, hop).wait_send()
+                back_copy(way, hop).wait_send()
+            return carry
+
+        lax.fori_loop(0, n - 1, relayed, 0)
 
     offsets[r] = offset_in[...]
 
@@ -295,23 +412,23 @@
 
             def left_part(j, carry):
                 g = (r // per + 1 + j) % LEFT_GROUPS
-                span = pl.ds(aligned(g * left_part_rows, left_part_rows), left_part_rows)
                 product = lax.dot_general(
-                    gain[span, :], cov_next[...], CONTRACT_LAST,
+                    gain[pl.ds(g * per, per)].reshape(left_part_rows, size),
+                    cov_next[...], CONTRACT_LAST,
                     preferred_element_type=jnp.float32,
                 ).astype(jnp.bfloat16)
                 for i in range(per):
                     d = g * per + i
-                    for way in range(2):
-                        top = i * rows + way * half
-                        store_block(left_out, d, way, product[top:top + half])
+                    for way in range(THIRDS):
+                        top = i * rows + way * third
+                        store_block(left_out, d, way, product[top:top + third])
 
                 def send(i, carry):
                     d = g * per + (r + i) % per
 
                     @pl.when(d != r)
                     def _():
-                        for way in range(2):
+                        for way in range(THIRDS):
                             left_copy(d, way).start()
 
                     return carry
@@ -326,13 +443,13 @@
         left[rows:, :] = jnp.broadcast_to(mean_next[...], (PAD, size)).astype(jnp.bfloat16)
 
         def await_left(i, carry):
-            for way in range(2):
+            for way in range(THIRDS):
                 left_arrival(ring_row((place + i) % n, n), way).wait_recv()
             return carry
 
         lax.fori_loop(1, n, await_left, 0)
         for d in range(n):
-            for way in range(2):
+            for way in range(THIRDS):
                 place_block(d, way)
 
         offsets[0] = whole_offset
@@ -340,7 +457,8 @@
         def right_part(j, carry):
             columns = pl.ds(aligned(j * part, part), part)
             product = lax.dot_general(
-                left[...], gain[columns, :], CONTRACT_LAST, preferred_element_type=jnp.float32
+                left[...], gain[pl.ds(j * (n // GROUPS), n // GROUPS)].reshape(part, size),
+                CONTRACT_LAST, preferred_element_type=jnp.float32,
             )
             cov_out[:, columns] = (
                 product[:rows] + cov_in[:, columns].astype(jnp.float32)
@@ -366,19 +484,11 @@
             store_cov(j).wait()
 
         def left_gone(i, carry):
-            for way in range(2):
+            for way in range(THIRDS):
                 left_copy(ring_row((place + i) % n, n), way).wait_send()
             return carry
 
         lax.fori_loop(1, n, left_gone, 0)
-
-        def ring_gone(hop, carry):
-            for c in range(CHUNKS):
-                for way in range(2):
-                    ring_copy(way, hop, c).wait_send()
-            return carry
-
-        lax.fori_loop(0, n - 1, ring_gone, 0)
 
     @pl.when(t > 0)
     def _():
@@ -404,7 +514,7 @@
     vmem = pl.BlockSpec(memory_space=pltpu.VMEM)
     hbm = pl.BlockSpec(memory_space=pl.ANY)
     lanes = main_lanes(rows)
-    folded = (n, 2, rows // 2 * rows // lanes, lanes)
+    folded = (n, THIRDS, rows // THIRDS * rows // lanes, lanes)
     dma = pltpu.SemaphoreType.DMA
     mean_row, cov = pl.pallas_call(
         functools.partial(kernel, steps, n),
@@ -415,7 +525,7 @@
         in_specs=[hbm, vmem, hbm],
         out_specs=(vmem, hbm),
         scratch_shapes=[
-            pltpu.VMEM((size, size), jnp.bfloat16),
+            pltpu.VMEM((n, rows, size), jnp.bfloat16),
             pltpu.VMEM((rows, size), jnp.bfloat16),
             pltpu.VMEM((rows, size), jnp.bfloat16),
             pltpu.VMEM((rows, size), jnp.bfloat16),
@@ -426,10 +536,10 @@
             pltpu.VMEM((1, size), jnp.float32),
             pltpu.VMEM((1, size), jnp.float32),
             dma,
-            dma((2, n, CHUNKS)),
-            dma((2, n, CHUNKS)),
-            dma((2, n)),
-            dma((2, n)),
+            dma((2, n, PIECES // 2)),
+            dma((2, n, PIECES // 2)),
+            dma((THIRDS, n)),
+            dma((THIRDS, n)),
             dma((n,)),
             dma((n,)),
             dma((GROUPS,)),
@@ -437,6 +547,13 @@
             dma((2,)),
             dma,
             dma((GROUPS,)),
+            pltpu.VMEM((n, 2, rows // PIECES, size), jnp.bfloat16),
+            dma((2,)),
+            dma((2,)),
+            dma((2, n)),
+            dma((2, n)),
+            dma((2, n)),
+            dma((2, n)),
             pltpu.SemaphoreType.REGULAR,
         ],
         compiler_params=pltpu.CompilerParams(

time: 86 us -> 97.9 us (1.14)
  Pallas kernels: 80.4 us -> 92.4 us
    pallas_call x1, Pallas kernels: 80.4 us -> 92.4 us  [shards(): pl.pallas_call(functools.partial(kernel, steps, n), out_shape=(jax.ShapeD...]
where the time goes in v3:
time: 97.9 us; the launch traced here: 97.7 us
  Pallas kernels  92.4 us (94%)
  local copies, waits for them, and re-layouts  4.64 us (5%)
    pallas_call x1, Pallas kernels, shards(): pl.pallas_call(functools.partial(kernel, steps, n), out_shape=(jax.ShapeD...  92.4 us
    unnamed x5, local copies, waits for them, and re-layouts  3.18 us

profile of v3, /device:TPU:0, one launch (start us, length us, event | category | flops | bytes accessed | tf_op | source)
XLA Modules:
  0.0 97.7 jit_solution(13003688208551992972)
XLA Ops:
  0.6 0.0 copy-start.1
  0.6 0.7 copy-done.1
  1.3 0.1 dynamic_update_slice.3.offset_in
  1.5 0.0 copy-start
  1.5 0.6 copy-done
  2.1 92.4 %shard_map.50 = (f32[1,1536]{1,0:T(1,128)}, bf16[192,1536]{1,0:T(8,128)(2,1)}) custom-call(bf16[192,1536]{1,0:T(8,128)(2,1)} %bitcast.3, f32[1,1536]{1,0:T(1,128)} %copy-done, bf16[192,1536]{1,0:T(8,128)(2,1)} %bitcast.4), custom_call_target="tpu_custom_call" | custom-call | tf_op jit(solution)/shard_map/pallas_call | solution.py:519
  94.5 1.3 %dynamic-slice_convert_fusion = bf16[1,192]{1,0:T(2,128)(2,1)} fusion(f32[1,1536]{1,0:T(1,128)} %get-tuple-element.4, s32[]{:T(128)S(6)} %select_n.4), kind=kLoop, calls=%fused_computation | loop fusion | bytes 772 | tf_op jit(solution)/shard_map/convert_element_type | solution.py:563
  95.8 1.9 %copy.7 = bf16[1,192,1536]{2,1,0:T(8,128)(2,1)} copy(bf16[1,192,1536]{2,1,0:T(8,128)(2,1)} %bitcast.5) | data formatting | bytes 1179648
  (2 shorter events, 0.0 us)
Async XLA Ops:
  0.6 0.7 copy-start.1
  1.5 0.6 copy-start

commit v4 on v2

--- a/solution.py
+++ b/solution.py
@@ -8,7 +8,7 @@
 from jax.sharding import PartitionSpec as P
 
 MESH = pl.DeviceIdType.MESH
-CHUNKS = 3
+PIECE = 16
 GROUPS = 4
 LEFT_GROUPS = 2
 HEAD_START = 2
@@ -31,17 +31,18 @@
 
 
 def kernel(
-    steps, n, gain_in, offset_in, cov_hbm, mean_out, cov_hbm_out,
-    gain, cov_in, cov_out, cov_next, left_out, left_in, left, offsets, mean_next, mean_send,
+    steps, n, gain_in, offset_in, cov_hbm, mean_out, cov_out,
+    gain, cov_in, cov_next, left_out, left_in, left, offsets, mean_next, mean_send,
     gain_sem, ring_send, ring_recv, left_send, left_recv,
-    offset_send, offset_recv, cov_send, cov_recv, mean_sems, cov_sem, out_sem, gate,
+    offset_send, offset_recv, cov_send, cov_recv, mean_sems, cov_sem, gate,
 ):
     t = lax.axis_index("tm")
     r = lax.axis_index("rows")
     place = ring_place(r, n)
     rows, size = cov_in.shape
     half = rows // 2
-    piece = half // CHUNKS
+    piece = PIECE
+    chunks = half // PIECE
     part = size // GROUPS
     left_part_rows = size // LEFT_GROUPS
     per = n // LEFT_GROUPS
@@ -58,12 +59,6 @@
     own_gain.start()
     own_cov = pltpu.make_async_copy(cov_hbm, cov_in, cov_sem)
     own_cov.start()
-
-    def store_cov(j):
-        columns = pl.ds(aligned(j * part, part), part)
-        return pltpu.make_async_copy(
-            cov_out.at[:, columns], cov_hbm_out.at[:, columns], out_sem.at[j]
-        )
 
     def store_block(ref, index, way, block):
         main = main_lanes(rows)
@@ -223,7 +218,7 @@
             def _():
                 pl.semaphore_wait(gate, 1)
 
-        for c in range(CHUNKS):
+        for c in range(chunks):
             for way in range(2):
                 ring_copy(way, 0, c).start()
 
@@ -234,7 +229,7 @@
                 store_block(left_in, r, way, left_half(r, way))
 
         def pass_on(hop, carry):
-            for c in range(CHUNKS):
+            for c in range(chunks):
                 for way in range(2):
                     ring_arrival(way, hop - 1, c).wait_recv()
                     ring_copy(way, hop, c).start()
@@ -256,7 +251,7 @@
 
         lax.fori_loop(1, n - 1, pass_on, 0)
 
-        for c in range(CHUNKS):
+        for c in range(chunks):
             for way in range(2):
                 ring_arrival(way, n - 2, c).wait_recv()
 
@@ -283,9 +278,7 @@
         mean_send[...] = whole_offset
         mean_copy().start()
         mean_out[...] = whole_offset
-        keep = pltpu.make_async_copy(cov_in, cov_hbm_out, cov_sem)
-        keep.start()
-        keep.wait()
+        cov_out[...] = cov_in[...]
 
     @pl.when(t < last)
     def _():
@@ -352,7 +345,6 @@
             def _():
                 cov_copy(cov_out, j).start()
 
-            store_cov(j).start()
             return carry
 
         lax.fori_loop(0, GROUPS, right_part, 0)
@@ -362,9 +354,6 @@
         def _():
             mean_copy().start()
 
-        for j in range(GROUPS):
-            store_cov(j).wait()
-
         def left_gone(i, carry):
             for way in range(2):
                 left_copy(ring_row((place + i) % n, n), way).wait_send()
@@ -373,7 +362,7 @@
         lax.fori_loop(1, n, left_gone, 0)
 
         def ring_gone(hop, carry):
-            for c in range(CHUNKS):
+            for c in range(chunks):
                 for way in range(2):
                     ring_copy(way, hop, c).wait_send()
             return carry
@@ -402,7 +391,7 @@
         jnp.zeros((1, size), jnp.float32), smoother_offsets.astype(jnp.float32), (0, start)
     )
     vmem = pl.BlockSpec(memory_space=pltpu.VMEM)
-    hbm = pl.BlockSpec(memory_space=pl.ANY)
+    hbm = pl.BlockSpec(memory_space=pltpu.HBM)
     lanes = main_lanes(rows)
     folded = (n, 2, rows // 2 * rows // lanes, lanes)
     dma = pltpu.SemaphoreType.DMA
@@ -413,10 +402,9 @@
             jax.ShapeDtypeStruct((rows, size), jnp.bfloat16),
         ),
         in_specs=[hbm, vmem, hbm],
-        out_specs=(vmem, hbm),
+        out_specs=(vmem, vmem),
         scratch_shapes=[
             pltpu.VMEM((size, size), jnp.bfloat16),
-            pltpu.VMEM((rows, size), jnp.bfloat16),
             pltpu.VMEM((rows, size), jnp.bfloat16),
             pltpu.VMEM((rows, size), jnp.bfloat16),
             pltpu.VMEM(folded, jnp.bfloat16),
@@ -426,8 +414,8 @@
             pltpu.VMEM((1, size), jnp.float32),
             pltpu.VMEM((1, size), jnp.float32),
             dma,
-            dma((2, n, CHUNKS)),
-            dma((2, n, CHUNKS)),
+            dma((2, n, rows // 2 // PIECE)),
+            dma((2, n, rows // 2 // PIECE)),
             dma((2, n)),
             dma((2, n)),
             dma((n,)),
@@ -436,13 +424,12 @@
             dma((GROUPS,)),
             dma((2,)),
             dma,
-            dma((GROUPS,)),
             pltpu.SemaphoreType.REGULAR,
         ],
         compiler_params=pltpu.CompilerParams(
-            collective_id=0, has_side_effects=True, vmem_limit_bytes=62 << 20
+            collective_id=0, has_side_effects=True, vmem_limit_bytes=40 << 20
         ),
-    )(own_gain, offset_row, own_cov)
+    )(pltpu.with_memory_space_constraint(own_gain, pltpu.HBM), offset_row, pltpu.with_memory_space_constraint(own_cov, pltpu.HBM))
     mean = lax.dynamic_slice(mean_row, (0, start), (1, rows)).astype(jnp.bfloat16)
     return mean, cov[None]
 

time: 86 us -> 82.6 us (0.960)
  local copies, waits for them, and re-layouts: 4.64 us -> 2.27 us
    unnamed x5 -> x3, local copies, waits for them, and re-layouts: 3.18 us -> 1.49 us
    pallas_call x1, Pallas kernels: 80.4 us -> 79.6 us  [shards(): pl.pallas_call(functools.partial(kernel, steps, n), out_shape=(jax.ShapeD...]
where the time goes in v4:
time: 82.6 us; the launch traced here: 82.5 us
  Pallas kernels  79.6 us (96%)
  local copies, waits for them, and re-layouts  2.27 us (3%)
    pallas_call x1, Pallas kernels, shards(): pl.pallas_call(functools.partial(kernel, steps, n), out_shape=(jax.ShapeD...  79.6 us

profile of v4, /device:TPU:0, one launch (start us, length us, event | category | flops | bytes accessed | tf_op | source)
XLA Modules:
  0.0 82.5 jit_solution(8886184159302214017)
XLA Ops:
  0.6 0.0 copy-start
  0.6 0.7 copy-done
  1.3 0.1 dynamic_update_slice.3.offset_in
  1.5 79.6 %shard_map.50 = (f32[1,1536]{1,0:T(1,128)S(1)}, bf16[192,1536]{1,0:T(8,128)(2,1)S(1)}) custom-call(bf16[192,1536]{1,0:T(8,128)(2,1)} %bitcast.4, f32[1,1536]{1,0:T(1,128)S(1)} %dynamic_update_slice.3.offset_in, bf16[192,1536]{1,0:T(8,128)(2,1)} %bitcast.5), custom_call_target="tpu_custom_call" | custom-call | tf_op jit(solution)/shard_map/pallas_call | solution.py:398
  81.0 0.6 dynamic-slice_convert_fusion
  81.7 0.8 copy.7
  (2 shorter events, 0.0 us)
Async XLA Ops:
  0.6 0.7 copy-start

commit v5 on v4

--- a/solution.py
+++ b/solution.py
@@ -34,7 +34,7 @@
     steps, n, gain_in, offset_in, cov_hbm, mean_out, cov_out,
     gain, cov_in, cov_next, left_out, left_in, left, offsets, mean_next, mean_send,
     gain_sem, ring_send, ring_recv, left_send, left_recv,
-    offset_send, offset_recv, cov_send, cov_recv, mean_sems, cov_sem, gate,
+    offset_send, offset_recv, cov_send, cov_recv, mean_sems, cov_sem, partial, gate,
 ):
     t = lax.axis_index("tm")
     r = lax.axis_index("rows")
@@ -318,22 +318,45 @@
         mean_copy().wait_recv()
         left[rows:, :] = jnp.broadcast_to(mean_next[...], (PAD, size)).astype(jnp.bfloat16)
 
-        def await_left(i, carry):
-            for way in range(2):
-                left_arrival(ring_row((place + i) % n, n), way).wait_recv()
+        near = r // per
+
+        def gather_half(h):
+            for i in range(per):
+                d = h * per + i
+
+                @pl.when(d != r)
+                def _():
+                    for way in range(2):
+                        left_arrival(d, way).wait_recv()
+
+            for g in range(LEFT_GROUPS):
+                @pl.when(h == g)
+                def _():
+                    for i in range(per):
+                        for way in range(2):
+                            place_block(g * per + i, way)
+
+            return pl.ds(aligned(h * left_part_rows, left_part_rows), left_part_rows)
+
+        near_inner = gather_half(near)
+
+        def near_part(j, carry):
+            columns = pl.ds(aligned(j * left_part_rows, left_part_rows), left_part_rows)
+            partial[:, columns] = lax.dot_general(
+                left[:, near_inner], gain[columns, near_inner], CONTRACT_LAST,
+                preferred_element_type=jnp.float32,
+            )
             return carry
 
-        lax.fori_loop(1, n, await_left, 0)
-        for d in range(n):
-            for way in range(2):
-                place_block(d, way)
-
+        lax.fori_loop(0, LEFT_GROUPS, near_part, 0)
+        far_inner = gather_half(1 - near)
         offsets[0] = whole_offset
 
         def right_part(j, carry):
             columns = pl.ds(aligned(j * part, part), part)
-            product = lax.dot_general(
-                left[...], gain[columns, :], CONTRACT_LAST, preferred_element_type=jnp.float32
+            product = partial[:, columns] + lax.dot_general(
+                left[:, far_inner], gain[columns, far_inner], CONTRACT_LAST,
+                preferred_element_type=jnp.float32,
             )
             cov_out[:, columns] = (
                 product[:rows] + cov_in[:, columns].astype(jnp.float32)
@@ -424,6 +447,7 @@
             dma((GROUPS,)),
             dma((2,)),
             dma,
+            pltpu.VMEM((rows + PAD, size), jnp.float32),
             pltpu.SemaphoreType.REGULAR,
         ],
         compiler_params=pltpu.CompilerParams(

time: 82.6 us -> 80.6 us (0.976)
  Pallas kernels: 79.6 us -> 77.5 us
    pallas_call x1, Pallas kernels: 79.6 us -> 77.5 us  [shards(): pl.pallas_call(functools.partial(kernel, steps, n), out_shape=(jax.ShapeD...]
where the time goes in v5:
time: 80.6 us; the launch traced here: 80.5 us
  Pallas kernels  77.5 us (96%)
  local copies, waits for them, and re-layouts  2.27 us (3%)
    pallas_call x1, Pallas kernels, shards(): pl.pallas_call(functools.partial(kernel, steps, n), out_shape=(jax.ShapeD...  77.5 us

profile of v5, /device:TPU:0, one launch (start us, length us, event | category | flops | bytes accessed | tf_op | source)
XLA Modules:
  0.0 80.5 jit_solution(4320703007713432290)
XLA Ops:
  0.6 0.0 copy-start
  0.6 0.7 copy-done
  1.3 0.1 dynamic_update_slice.3.offset_in
  1.5 77.5 %shard_map.50 = (f32[1,1536]{1,0:T(1,128)S(1)}, bf16[192,1536]{1,0:T(8,128)(2,1)S(1)}) custom-call(bf16[192,1536]{1,0:T(8,128)(2,1)} %bitcast.4, f32[1,1536]{1,0:T(1,128)S(1)} %dynamic_update_slice.3.offset_in, bf16[192,1536]{1,0:T(8,128)(2,1)} %bitcast.5), custom_call_target="tpu_custom_call" | custom-call | tf_op jit(solution)/shard_map/pallas_call | solution.py:421
  79.0 0.6 dynamic-slice_convert_fusion
  79.7 0.8 %copy.7 = bf16[1,192,1536]{2,1,0:T(8,128)(2,1)} copy(bf16[1,192,1536]{2,1,0:T(8,128)(2,1)S(1)} %bitcast.3) | data formatting | bytes 1179648
  (2 shorter events, 0.0 us)
Async XLA Ops:
  0.6 0.7 copy-start

commit v6 on v5

--- a/solution.py
+++ b/solution.py
@@ -11,7 +11,7 @@
 PIECE = 16
 GROUPS = 4
 LEFT_GROUPS = 2
-HEAD_START = 2
+HEAD_START = 1
 PAD = 16
 CONTRACT_LAST = (((1,), (1,)), ((), ()))
 

time: 80.6 us -> 80.6 us (level)
  no operation moved by 1% of the time
where the time goes in v6:
time: 80.6 us; the launch traced here: 80.5 us
  Pallas kernels  77.5 us (96%)
  local copies, waits for them, and re-layouts  2.27 us (3%)
    pallas_call x1, Pallas kernels, shards(): pl.pallas_call(functools.partial(kernel, steps, n), out_shape=(jax.ShapeD...  77.5 us

profile of v6, /device:TPU:0, one launch (start us, length us, event | category | flops | bytes accessed | tf_op | source)
XLA Modules:
  0.0 80.5 jit_solution(14838813573954917378)
XLA Ops:
  0.6 0.0 copy-start
  0.6 0.7 copy-done
  1.3 0.1 dynamic_update_slice.3.offset_in
  1.5 77.5 %shard_map.50 = (f32[1,1536]{1,0:T(1,128)S(1)}, bf16[192,1536]{1,0:T(8,128)(2,1)S(1)}) custom-call(bf16[192,1536]{1,0:T(8,128)(2,1)} %bitcast.4, f32[1,1536]{1,0:T(1,128)S(1)} %dynamic_update_slice.3.offset_in, bf16[192,1536]{1,0:T(8,128)(2,1)} %bitcast.5), custom_call_target="tpu_custom_call" | custom-call | tf_op jit(solution)/shard_map/pallas_call | solution.py:421
  79.0 0.6 dynamic-slice_convert_fusion
  79.7 0.8 %copy.7 = bf16[1,192,1536]{2,1,0:T(8,128)(2,1)} copy(bf16[1,192,1536]{2,1,0:T(8,128)(2,1)S(1)} %bitcast.3) | data formatting | bytes 1179648
  (2 shorter events, 0.0 us)
Async XLA Ops:
  0.6 0.7 copy-start

commit v7 on v5

--- a/solution.py
+++ b/solution.py
@@ -9,7 +9,7 @@
 
 MESH = pl.DeviceIdType.MESH
 PIECE = 16
-GROUPS = 4
+GROUPS = 3
 LEFT_GROUPS = 2
 HEAD_START = 2
 PAD = 16

time: 80.6 us -> 80.1 us (level)
  no operation moved by 1% of the time
where the time goes in v7:
time: 80.1 us; the launch traced here: 79.9 us
  Pallas kernels  77 us (96%)
  local copies, waits for them, and re-layouts  2.27 us (3%)
    pallas_call x1, Pallas kernels, shards(): pl.pallas_call(functools.partial(kernel, steps, n), out_shape=(jax.ShapeD...  77 us

profile of v7, /device:TPU:0, one launch (start us, length us, event | category | flops | bytes accessed | tf_op | source)
XLA Modules:
  0.0 79.9 jit_solution(8020937653399724526)
XLA Ops:
  0.6 0.0 copy-start
  0.6 0.7 copy-done
  1.3 0.1 dynamic_update_slice.3.offset_in
  1.5 77.0 %shard_map.50 = (f32[1,1536]{1,0:T(1,128)S(1)}, bf16[192,1536]{1,0:T(8,128)(2,1)S(1)}) custom-call(bf16[192,1536]{1,0:T(8,128)(2,1)} %bitcast.4, f32[1,1536]{1,0:T(1,128)S(1)} %dynamic_update_slice.3.offset_in, bf16[192,1536]{1,0:T(8,128)(2,1)} %bitcast.5), custom_call_target="tpu_custom_call" | custom-call | tf_op jit(solution)/shard_map/pallas_call | solution.py:421
  78.5 0.6 dynamic-slice_convert_fusion
  79.1 0.8 %copy.7 = bf16[1,192,1536]{2,1,0:T(8,128)(2,1)} copy(bf16[1,192,1536]{2,1,0:T(8,128)(2,1)S(1)} %bitcast.3) | data formatting | bytes 1179648
  (2 shorter events, 0.0 us)
Async XLA Ops:
  0.6 0.7 copy-start
